TPU v7x, 512 devices: a whole 4x8x8 slice. The times are simulated.
512 devices in a mesh: dp: 32 (over x, y), expert: 2 (over core), ffn: 8 (over z).
Axes of the slice: x: 4, y: 8, z: 8, core: 2. Of those that a mesh axis runs over, the one named last changes fastest.
Arguments:
- grad_rows: bfloat16 [4096, 6144], P('dp', 'ffn'), may hold values from -80 to 80
- gate_probs: float32 [4096, 2], P('dp'), may hold values from 0.1 to 1
- expert_ids: int32 [4096, 2], P('dp'), may hold values from 0 to 3, all different within a row; in each aligned block of 128 rows (0 to 127, 128 to 255, ...) at most 72 rows name the same one
- gate_pre: bfloat16 [4, 2304, 8192], P('expert', 'ffn', 'dp'), may hold values from -6 to 6
- up_pre: bfloat16 [4, 2304, 8192], P('expert', 'ffn', 'dp'), may hold values from -40 to 40
- down_weight: bfloat16 [4, 8192, 6144], P('expert', 'dp', 'ffn'), may hold values from -0.0625 to 0.0625
Outputs:
- down_grad: bfloat16 [4, 8192, 6144], P('expert', 'dp', 'ffn')
- gate_grad: bfloat16 [4, 2304, 8192], P('expert', 'ffn', 'dp')
- up_grad: bfloat16 [4, 2304, 8192], P('expert', 'ffn', 'dp')
Inputs may be any that keep to these rules, and one draw needn't show every extreme that they name: `expert_ids`: in the 128 tokens of one index of dp no expert is named by more than 72 routes, a bound that some block reaches; a token's two routes name different experts.
All inputs are finite; a program needn't handle non-finite values.
Results may differ from a plain program's by a relative error of at most 0.019.
Values may be sent and summed in bfloat16 or wider, within the bound.
No kernel may reach another device: no remote copies, remote signals or barrier semaphores. Data moves between devices by JAX's collectives and lax.ppermute only.
A program may use at most 64 MiB of HBM per device.

v0:
```python
import math
import jax
import jax.numpy as jnp
from jax import lax
from jax.sharding import PartitionSpec as P

CAP = 72


def slot_table(route_ids, experts_total):
    tokens_here, routes = route_ids.shape
    flat_ids = route_ids.reshape(tokens_here * routes)
    one_hot = (flat_ids[:, None] == jnp.arange(experts_total, dtype=jnp.int32)[None, :]).astype(
        jnp.int32
    )
    earlier = jnp.cumsum(one_hot, axis=0) - one_hot
    return jnp.sum(earlier * one_hot, axis=1).reshape(tokens_here, routes)


def on_device(grad_rows, gate_probs, expert_ids, gate_pre, up_pre, down_weight):
    experts_here, rows_here, hidden_width = gate_pre.shape
    feature_width = down_weight.shape[2]
    capacity = CAP
    experts_total = experts_here * lax.axis_size("expert")
    slot_index = slot_table(expert_ids, experts_total)
    first_expert = lax.axis_index("expert") * experts_here
    local_ids = expert_ids - first_expert
    expert_match = (
        local_ids[:, :, None] == jnp.arange(experts_here, dtype=jnp.int32)[None, None, :]
    ).astype(jnp.float32)
    expert_match = expert_match * gate_probs[:, :, None]
    slot_match = (
        slot_index[:, :, None] == jnp.arange(capacity, dtype=jnp.int32)[None, None, :]
    ).astype(jnp.float32)
    placing = jnp.einsum("tke,tks->est", expert_match, slot_match, precision=lax.Precision.HIGHEST)
    dispatched = jnp.einsum(
        "est,td->esd", placing, grad_rows.astype(jnp.float32), precision=lax.Precision.HIGHEST
    ).astype(jnp.bfloat16)
    arrived = lax.all_gather(dispatched, "dp", axis=1, tiled=True)
    gate_value = gate_pre.astype(jnp.float32)
    up_value = up_pre.astype(jnp.float32)
    sigmoid_gate = jax.nn.sigmoid(gate_value)
    silu_gate = gate_value * sigmoid_gate
    hidden = (silu_gate * up_value).astype(jnp.bfloat16)
    partial_sums = jnp.einsum(
        "erd,efd->erf", arrived, down_weight, preferred_element_type=jnp.float32
    )
    own_rows = lax.psum_scatter(
        partial_sums.astype(jnp.bfloat16), "ffn", scatter_dimension=1, tiled=True
    ).astype(jnp.float32)
    gate_grad = (
        own_rows * up_value * sigmoid_gate * (1.0 + gate_value * (1.0 - sigmoid_gate))
    ).astype(jnp.bfloat16)
    up_grad = (own_rows * silu_gate).astype(jnp.bfloat16)
    weight_grad = jnp.einsum(
        "erf,erd->efd",
        lax.all_gather(hidden, "ffn", axis=1, tiled=True),
        arrived,
        preferred_element_type=jnp.float32,
    )
    squares = lax.psum(jnp.sum(weight_grad * weight_grad), ("dp", "expert", "ffn"))
    entry_count = (
        float(experts_total)
        * float(hidden_width * lax.axis_size("dp"))
        * float(feature_width * lax.axis_size("ffn"))
    )
    clip_limit = jnp.float32(0.5 * math.sqrt(entry_count))
    factor = clip_limit / jnp.maximum(jnp.sqrt(squares), clip_limit)
    down_grad = (weight_grad * factor).astype(jnp.bfloat16)
    return (down_grad, gate_grad, up_grad)


def solution(mesh):
    placed = (
        P("dp", "ffn"),
        P("dp", None),
        P("dp", None),
        P("expert", "ffn", "dp"),
        P("expert", "ffn", "dp"),
        P("expert", "dp", "ffn"),
    )
    return jax.shard_map(
        on_device,
        mesh=mesh,
        in_specs=placed,
        out_specs=(P("expert", "dp", "ffn"), P("expert", "ffn", "dp"), P("expert", "ffn", "dp")),
        check_vma=False,
    )
```

profile of v0, /device:TPU:1, one launch (start us, length us, event | category | flops | bytes accessed | tf_op | source)
XLA Modules:
  0.0 325.6 jit_solution(6122541284965118763)
XLA Ops:
  7.2 0.0 copy-start
  7.2 0.0 copy-start.3
  7.2 0.0 all-gather.5.cloned.1.call-start
  7.2 0.9 copy.13
  8.1 0.1 eq.57
  8.3 0.1 eq.53
  8.4 0.7 broadcast_subtract_fusion
  9.1 0.1 copy.17
  9.2 1.2 reduce-window.6
  10.4 0.1 slice.8
  10.5 0.1 copy.15
  10.7 0.1 copy.16
  10.8 0.1 add_bitcast_fusion
  10.9 0.1 eq.61
  11.0 0.8 copy.18
  11.8 1.1 fusion.9
  12.9 0.1 copy.19
  13.0 0.0 copy-done.3
  13.0 1.0 convolution_convert_fusion.1
  14.1 0.0 all-gather.5.cloned.1.call-update
  14.1 0.0 reduce-scatter.2.cloned.1.call-start
  14.1 102.3 %all-gather.5.cloned.1.call-done = bf16[2,2304,768]{2,1,0:T(8,128)(2,1)} async-done(((bf16[2,72,768]{2,1,0:T(8,128)(2,1)}), bf16[2,2304,768]{2,1,0:T(8,128)(2,1)}) %all-gather.5.cloned.1.call-update) | async-done | bytes 7077904 | tf_op jit(solution)/shard_map/all_gather | solution.py:39
  116.4 0.0 copy-done
  116.4 6.5 %convolution_convert_fusion = bf16[2,2304,256]{2,1,0:T(8,128)(2,1)} fusion(bf16[2,2304,768]{2,1,0:T(8,128)(2,1)} %all-gather.5.cloned.1.call-done, bf16[2,256,768]{2,1,0:T(8,128)(2,1)S(1)} %copy-done), kind=kOutput, calls=%fused_computation | convolution fusion | flops 1813118976 | bytes 10223616 | tf_op jit(solution)/shard_map/erd,efd->erf/dot_general | solution.py:45
  123.0 0.0 copy-start.1
  123.0 0.0 copy-start.2
  123.0 0.0 reduce-scatter.2.cloned.1.call-update
  123.0 0.0 all-gather.3.cloned.1.call-start
  123.0 40.2 %reduce-scatter.2.cloned.1.call-done = bf16[2,288,256]{2,1,0:T(8,128)(2,1)} async-done(((bf16[2,2304,256]{2,1,0:T(8,128)(2,1)}), bf16[2,288,256]{2,1,0:T(8,128)(2,1)}) %reduce-scatter.2.cloned.1.call-update) | async-done | bytes 294928 | tf_op jit(solution)/shard_map/reduce_scatter | solution.py:48
  163.3 0.0 copy-done.1
  163.3 0.0 copy-done.2
  163.3 2.3 fusion.4
  165.6 0.0 all-gather.3.cloned.1.call-update
  165.6 45.2 %all-gather.3.cloned.1.call-done = bf16[2,2304,256]{2,1,0:T(8,128)(2,1)} async-done(((bf16[2,288,256]{2,1,0:T(8,128)(2,1)}), bf16[2,2304,256]{2,1,0:T(8,128)(2,1)}) %all-gather.3.cloned.1.call-update) | async-done | bytes 2359312 | tf_op jit(solution)/shard_map/all_gather | solution.py:57
  210.9 6.5 %multiply_reduce_fusion = (f32[]{:T(128)}, f32[2,256,768]{2,1,0:T(8,128)S(1)}) fusion(bf16[2,2304,256]{2,1,0:T(8,128)(2,1)} %all-gather.3.cloned.1.call-done, bf16[2,2304,768]{2,1,0:T(8,128)(2,1)} %all-gather.5.cloned.1.call-done), kind=kOutput, calls=%fused_computation.2 | convolution fusion | flops 1812725760 | bytes 11010052 | tf_op jit(solution)/shard_map/erf,erd->efd/dot_general | solution.py:55
  217.4 100.0 %psum.7 = f32[]{:T(128)} all-reduce(f32[]{:T(128)} %get-tuple-element.6), channel_id=1, replica_groups=mesh['dp'=32,'expert'=2,'ffn'=8] {'dp','expert','ffn'}, use_global_device_ids=true, to_apply=%region_4.5 | all-reduce | flops 1 | bytes 8 | tf_op jit(solution)/shard_map/psum | solution.py:61
  318.1 1.0 multiply_convert_fusion
  (4 shorter events, 0.1 us)
Async XLA Ops:
  7.2 109.3 %copy-start = (bf16[2,256,768]{2,1,0:T(8,128)(2,1)S(1)}, bf16[2,256,768]{2,1,0:T(8,128)(2,1)}, u32[]{:S(2)}) copy-start(bf16[2,256,768]{2,1,0:T(8,128)(2,1)} %param.11) | copy-start | bytes 2359300
  7.2 5.9 %copy-start.3 = (bf16[128,768]{1,0:T(8,128)(2,1)S(1)}, bf16[128,768]{1,0:T(8,128)(2,1)}, u32[]{:S(2)}) copy-start(bf16[128,768]{1,0:T(8,128)(2,1)} %param.6) | copy-start | bytes 589828
  7.2 109.3 %all-gather.5.cloned.1.call-start = ((), (), s32[]{:S(2)}) async-start(), calls=%async_computation.2 | async-start | bytes 7299072 | tf_op jit(solution)/shard_map/all_gather | solution.py:39
  14.1 149.2 %reduce-scatter.2.cloned.1.call-start = ((), (), s32[]{:S(2)}) async-start(), calls=%async_computation.3 | async-start | bytes 2654208 | tf_op jit(solution)/shard_map/reduce_scatter | solution.py:48
  123.0 40.3 %copy-start.1 = (bf16[2,288,256]{2,1,0:T(8,128)(2,1)S(1)}, bf16[2,288,256]{2,1,0:T(8,128)(2,1)}, u32[]{:S(2)}) copy-start(bf16[2,288,256]{2,1,0:T(8,128)(2,1)} %param.9) | copy-start | bytes 884740
  123.0 40.3 %copy-start.2 = (bf16[2,288,256]{2,1,0:T(8,128)(2,1)S(1)}, bf16[2,288,256]{2,1,0:T(8,128)(2,1)}, u32[]{:S(2)}) copy-start(bf16[2,288,256]{2,1,0:T(8,128)(2,1)} %param.10) | copy-start | bytes 884740
  123.0 87.9 %all-gather.3.cloned.1.call-start = ((), (), s32[]{:S(2)}) async-start(), calls=%async_computation.1 | async-start | bytes 2654208 | tf_op jit(solution)/shard_map/all_gather | solution.py:57
Sparse Core Ops, SparseCore 0:
  14.2 102.1 all-gather.4
  123.1 40.1 reduce-scatter.1
  165.9 44.8 all-gather.2
where the time goes:
time: 326 us
  waiting for transfers between devices  188 us (58%)
  blocking collectives  100 us (31%)
  matrix products  15.2 us (5%)
  between operations  14.5 us (4%)
  other arithmetic  5.35 us (2%)
    all_gather x1, waiting for transfers between devices, on_device(): arrived = lax.all_gather(dispatched, 'dp', axis=1, tiled=True)  102 us
    psum x1, blocking collectives, on_device(): lax.psum(jnp.sum(weight_grad * weight_grad), ('dp', 'expert', 'ffn'))  100 us
    all_gather x1, waiting for transfers between devices, on_device(): lax.all_gather(hidden, 'ffn', axis=1, tiled=True)  45.2 us
    reduce_scatter x1, waiting for transfers between devices, on_device(): lax.psum_scatter(partial_sums.astype(jnp.bfloat16), 'ffn', scatter_dimens...  40.2 us
    dot_general x1, matrix products, on_device(): jnp.einsum('erf,erd->efd', lax.all_gather(hidden, 'ffn', axis=1, tiled=Tr...  6.55 us
  transfers between devices with their start and end apart: 3, of which 3 were waited for; matrix products, arithmetic and copies ran while one was open for 0% of the time, Pallas kernels for 0%

commit v1 on v0

--- a/solution.py
+++ b/solution.py
@@ -52,11 +52,30 @@
         own_rows * up_value * sigmoid_gate * (1.0 + gate_value * (1.0 - sigmoid_gate))
     ).astype(jnp.bfloat16)
     up_grad = (own_rows * silu_gate).astype(jnp.bfloat16)
-    weight_grad = jnp.einsum(
-        "erf,erd->efd",
-        lax.all_gather(hidden, "ffn", axis=1, tiled=True),
-        arrived,
-        preferred_element_type=jnp.float32,
+
+    def strips_all_supply(t0, xs):
+        x_now, carry_in, back = (jax.lax.psum(1, "ffn"), jax.lax.axis_index("ffn"), t0.shape[1])
+        queue = [(nth, (nth + 1) % x_now) for nth in range(x_now)]
+        all_rows = [(nth, (nth - 1) % x_now) for nth in range(x_now)]
+        reached = x_now // 2
+        ready = row_out = t0
+        out_arr = xs(t0, carry_in * back)
+        for t in range(1, reached + 1):
+            ready = jax.lax.ppermute(ready, "ffn", queue)
+            if t < x_now - reached:
+                row_out = jax.lax.ppermute(row_out, "ffn", perm=all_rows)
+                out_arr = out_arr + xs(row_out, (carry_in + t) % x_now * back)
+            out_arr = out_arr + xs(ready, (carry_in - t) % x_now * back)
+        return out_arr
+
+    weight_grad = strips_all_supply(
+        hidden,
+        lambda part, offset: jnp.einsum(
+            "erf,erd->efd",
+            part,
+            lax.dynamic_slice_in_dim(arrived, offset, part.shape[1], axis=1),
+            preferred_element_type=jnp.float32,
+        ),
     )
     squares = lax.psum(jnp.sum(weight_grad * weight_grad), ("dp", "expert", "ffn"))
     entry_count = (

time: 326 us -> 319 us (0.979)
  waiting for transfers between devices: 188 us -> 151 us
  starting transfers between devices: 0.12 us -> 21.6 us
  blocking collectives: 100 us -> 105 us
    all_gather x1 -> x0, waiting for transfers between devices: 45.2 us -> none  [on_device(): lax.all_gather(hidden, 'ffn', axis=1, tiled=True)]
    ppermute x0 -> x7, starting transfers between devices: none -> 21.5 us  [the longest x3 13.4 us: strips_all_supply(): row_out = jax.lax.ppermute(row_out, 'ffn', perm=all_rows)]
    ppermute x0 -> x7, waiting for transfers between devices: none -> 7.75 us  [the longest x4 7.74 us: strips_all_supply(): ready = jax.lax.ppermute(ready, 'ffn', queue)]
    psum x1, blocking collectives: 100 us -> 105 us  [on_device(): lax.psum(jnp.sum(weight_grad * weight_grad), ('dp', 'expert', 'ffn'))]
    dot_general x1 -> x8, matrix products: 6.55 us -> 9.71 us  [on_device(): jnp.einsum('erf,erd->efd', part, lax.dynamic_slice_in_dim(arrived, offset...]
  transfers between devices with their start and end apart: 3 -> 9, of which waited for: 3 -> 5; matrix products, arithmetic and copies ran while one was open for 0% -> 3% of each run, Pallas kernels for 0% -> 0%
where the time goes in v1:
time: 319 us
  waiting for transfers between devices  151 us (47%)
  blocking collectives  105 us (33%)
  starting transfers between devices  21.6 us (7%)
  matrix products  18.4 us (6%)
  between operations  15.1 us (5%)
  other arithmetic  5.17 us (2%)
    psum x1, blocking collectives, on_device(): lax.psum(jnp.sum(weight_grad * weight_grad), ('dp', 'expert', 'ffn'))  105 us
    all_gather x1, waiting for transfers between devices, on_device(): arrived = lax.all_gather(dispatched, 'dp', axis=1, tiled=True)  102 us
    reduce_scatter x1, waiting for transfers between devices, on_device(): lax.psum_scatter(partial_sums.astype(jnp.bfloat16), 'ffn', scatter_dimens...  40.7 us
    ppermute x3, starting transfers between devices, strips_all_supply(): row_out = jax.lax.ppermute(row_out, 'ffn', perm=all_rows)  13.4 us
    dot_general x8, matrix products, on_device(): jnp.einsum('erf,erd->efd', part, lax.dynamic_slice_in_dim(arrived, offset...  9.71 us
    ppermute x4, starting transfers between devices, strips_all_supply(): ready = jax.lax.ppermute(ready, 'ffn', queue)  8.1 us
    ppermute x4, waiting for transfers between devices, strips_all_supply(): ready = jax.lax.ppermute(ready, 'ffn', queue)  7.74 us
    dot_general x1, matrix products, on_device(): jnp.einsum('erd,efd->erf', arrived, down_weight, preferred_element_type=j...  6.51 us
  transfers between devices with their start and end apart: 9, of which 5 were waited for; matrix products, arithmetic and copies ran while one was open for 3% of the time, Pallas kernels for 0%

profile of v1, /device:TPU:1, one launch (start us, length us, event | category | flops | bytes accessed | tf_op | source)
XLA Modules:
  0.0 318.6 jit_solution(17496911375060153053)
XLA Ops:
  7.2 0.0 copy-start
  7.2 0.0 all-gather.2.cloned.1.call-start
  7.2 0.8 copy.13
  8.1 0.1 eq.65
  8.2 0.1 eq.61
  8.4 0.7 broadcast_subtract_fusion
  9.1 0.1 copy.17
  9.2 1.2 reduce-window.6
  10.4 0.1 slice.8
  10.5 0.1 copy.15
  10.6 0.1 copy.16
  10.7 0.1 add_bitcast_fusion
  10.8 0.1 eq.69
  11.0 0.8 copy.18
  11.7 0.0 copy-start.4
  11.8 1.1 fusion.24
  12.9 0.1 copy.19
  13.0 0.0 copy-done.4
  13.0 1.0 convolution_convert_fusion.1
  14.0 0.0 all-gather.2.cloned.1.call-update
  14.0 0.0 reduce-scatter.2.cloned.1.call-start
  14.1 102.3 %all-gather.2.cloned.1.call-done = bf16[2,2304,768]{2,1,0:T(8,128)(2,1)} async-done(((bf16[2,72,768]{2,1,0:T(8,128)(2,1)}), bf16[2,2304,768]{2,1,0:T(8,128)(2,1)}) %all-gather.2.cloned.1.call-update) | async-done | bytes 7077904 | tf_op jit(solution)/shard_map/all_gather | solution.py:39
  116.4 0.0 copy-done
  116.4 6.5 %convolution_convert_fusion = bf16[2,2304,256]{2,1,0:T(8,128)(2,1)} fusion(bf16[2,2304,768]{2,1,0:T(8,128)(2,1)} %all-gather.2.cloned.1.call-done, bf16[2,256,768]{2,1,0:T(8,128)(2,1)S(1)} %copy-done), kind=kOutput, calls=%fused_computation | convolution fusion | flops 1813118976 | bytes 10223616 | tf_op jit(solution)/shard_map/erd,efd->erf/dot_general | solution.py:45
  122.9 0.0 copy-start.2
  122.9 0.0 copy-start.3
  122.9 0.0 reduce-scatter.2.cloned.1.call-update
  122.9 40.7 %reduce-scatter.2.cloned.1.call-done = bf16[2,288,256]{2,1,0:T(8,128)(2,1)} async-done(((bf16[2,2304,256]{2,1,0:T(8,128)(2,1)}), bf16[2,288,256]{2,1,0:T(8,128)(2,1)}) %reduce-scatter.2.cloned.1.call-update) | async-done | bytes 294928 | tf_op jit(solution)/shard_map/reduce_scatter | solution.py:48
  163.6 0.0 copy-done.2
  163.6 0.0 copy-done.3
  163.6 2.1 fusion.19
  165.8 2.2 collective-permute-start.1
  168.0 4.3 %collective-permute-start = (bf16[2,288,256]{2,1,0:T(8,128)(2,1)S(1)}, bf16[2,288,256]{2,1,0:T(8,128)(2,1)S(1)}, u32[]{:S(2)}, u32[]{:S(2)}) collective-permute-start(bf16[2,288,256]{2,1,0:T(8,128)(2,1)S(1)} %get-tuple-element.5), channel_id=1, source_target_pairs={{0,7},{1,0},{2,1},{3,2},{4,3},{5,4},{6,5},{7,6},{8,15},{9,8},{10,9... | collective-permute-start | bytes 884744 | tf_op jit(solution)/shard_map/ppermute | solution.py:66
  172.4 0.0 copy-start.1
  172.4 1.9 fusion.13
  174.4 0.1 collective-permute-done.1
  174.4 2.0 collective-permute-start.3
  176.5 0.0 collective-permute-done
  176.5 4.6 %collective-permute-start.2 = (bf16[2,288,256]{2,1,0:T(8,128)(2,1)S(1)}, bf16[2,288,256]{2,1,0:T(8,128)(2,1)S(1)}, u32[]{:S(2)}, u32[]{:S(2)}) collective-permute-start(bf16[2,288,256]{2,1,0:T(8,128)(2,1)S(1)} %collective-permute-done), channel_id=1, source_target_pairs={{0,7},{1,0},{2,1},{3,2},{4,3},{5,4},{6,5},{7,6},{8,15},{9,8},{10,9... | collective-permute-start | bytes 884744 | tf_op jit(solution)/shard_map/ppermute | solution.py:66
  181.1 1.8 fusion.11
  182.9 1.8 fusion.9
  184.7 0.0 collective-permute-done.3
  184.7 1.9 collective-permute-start.5
  186.6 0.0 collective-permute-done.2
  186.6 4.6 %collective-permute-start.4 = (bf16[2,288,256]{2,1,0:T(8,128)(2,1)S(1)}, bf16[2,288,256]{2,1,0:T(8,128)(2,1)S(1)}, u32[]{:S(2)}, u32[]{:S(2)}) collective-permute-start(bf16[2,288,256]{2,1,0:T(8,128)(2,1)S(1)} %collective-permute-done.2), channel_id=1, source_target_pairs={{0,7},{1,0},{2,1},{3,2},{4,3},{5,4},{6,5},{7,6},{8,15},{9,8},{10,9... | collective-permute-start | bytes 884744 | tf_op jit(solution)/shard_map/ppermute | solution.py:66
  191.2 0.0 copy-done.1
  191.2 0.6 fusion.7
  191.9 0.6 fusion.5
  192.5 0.9 collective-permute-done.5
  193.4 1.9 collective-permute-start.6
  195.3 0.6 fusion.1
  195.9 0.0 collective-permute-done.4
  195.9 0.6 fusion.3
  196.6 6.8 %collective-permute-done.6 = bf16[2,288,256]{2,1,0:T(8,128)(2,1)S(1)} collective-permute-done((bf16[2,288,256]{2,1,0:T(8,128)(2,1)S(1)}, bf16[2,288,256]{2,1,0:T(8,128)(2,1)S(1)}, u32[]{:S(2)}, u32[]{:S(2)}) %collective-permute-start.6) | collective-permute-done | bytes 294944 | tf_op jit(solution)/shard_map/ppermute | solution.py:64
  203.4 1.6 multiply_reduce_fusion
  205.0 105.1 %psum.7 = f32[]{:T(128)} all-reduce(f32[]{:T(128)} %get-tuple-element.6), channel_id=1, replica_groups=mesh['dp'=32,'expert'=2,'ffn'=8] {'dp','expert','ffn'}, use_global_device_ids=true, to_apply=%region_4.5 | all-reduce | flops 1 | bytes 8 | tf_op jit(solution)/shard_map/psum | solution.py:80
  310.8 1.0 multiply_convert_fusion
  (4 shorter events, 0.1 us)
Async XLA Ops:
  7.2 109.2 %copy-start = (bf16[2,256,768]{2,1,0:T(8,128)(2,1)S(1)}, bf16[2,256,768]{2,1,0:T(8,128)(2,1)}, u32[]{:S(2)}) copy-start(bf16[2,256,768]{2,1,0:T(8,128)(2,1)} %param.11) | copy-start | bytes 2359300
  7.2 109.2 %all-gather.2.cloned.1.call-start = ((), (), s32[]{:S(2)}) async-start(), calls=%async_computation.1 | async-start | bytes 7299072 | tf_op jit(solution)/shard_map/all_gather | solution.py:39
  11.7 1.2 copy-start.4
  14.0 149.6 %reduce-scatter.2.cloned.1.call-start = ((), (), s32[]{:S(2)}) async-start(), calls=%async_computation.2 | async-start | bytes 2654208 | tf_op jit(solution)/shard_map/reduce_scatter | solution.py:48
  122.9 40.7 %copy-start.2 = (bf16[2,288,256]{2,1,0:T(8,128)(2,1)S(1)}, bf16[2,288,256]{2,1,0:T(8,128)(2,1)}, u32[]{:S(2)}) copy-start(bf16[2,288,256]{2,1,0:T(8,128)(2,1)} %param.9) | copy-start | bytes 884740
  122.9 40.7 %copy-start.3 = (bf16[2,288,256]{2,1,0:T(8,128)(2,1)S(1)}, bf16[2,288,256]{2,1,0:T(8,128)(2,1)}, u32[]{:S(2)}) copy-start(bf16[2,288,256]{2,1,0:T(8,128)(2,1)} %param.10) | copy-start | bytes 884740
  165.8 8.7 %collective-permute-start.1 = (bf16[2,288,256]{2,1,0:T(8,128)(2,1)S(1)}, bf16[2,288,256]{2,1,0:T(8,128)(2,1)S(1)}, u32[]{:S(2)}, u32[]{:S(2)}) collective-permute-start(bf16[2,288,256]{2,1,0:T(8,128)(2,1)S(1)} %get-tuple-element.5), channel_id=1, source_target_pairs={{0,1},{1,2},{2,3},{3,4},{4,5},{5,6},{6,7},{7,0},{8,9},{9,10},{10,1... | collective-permute-start | bytes 884744 | tf_op jit(solution)/shard_map/ppermute | solution.py:64
  168.0 8.5 %collective-permute-start = (bf16[2,288,256]{2,1,0:T(8,128)(2,1)S(1)}, bf16[2,288,256]{2,1,0:T(8,128)(2,1)S(1)}, u32[]{:S(2)}, u32[]{:S(2)}) collective-permute-start(bf16[2,288,256]{2,1,0:T(8,128)(2,1)S(1)} %get-tuple-element.5), channel_id=1, source_target_pairs={{0,7},{1,0},{2,1},{3,2},{4,3},{5,4},{6,5},{7,6},{8,15},{9,8},{10,9... | collective-permute-start | bytes 884744 | tf_op jit(solution)/shard_map/ppermute | solution.py:66
  172.4 18.8 %copy-start.1 = (bf16[2,2304,768]{2,1,0:T(8,128)(2,1)S(1)}, bf16[2,2304,768]{2,1,0:T(8,128)(2,1)}, u32[]{:S(2)}) copy-start(bf16[2,2304,768]{2,1,0:T(8,128)(2,1)} %all-gather.2.cloned.1.call-done) | copy-start | bytes 21233668
  174.4 10.3 %collective-permute-start.3 = (bf16[2,288,256]{2,1,0:T(8,128)(2,1)S(1)}, bf16[2,288,256]{2,1,0:T(8,128)(2,1)S(1)}, u32[]{:S(2)}, u32[]{:S(2)}) collective-permute-start(bf16[2,288,256]{2,1,0:T(8,128)(2,1)S(1)} %collective-permute-done.1), channel_id=1, source_target_pairs={{0,1},{1,2},{2,3},{3,4},{4,5},{5,6},{6,7},{7,0},{8,9},{9,10},{10,1... | collective-permute-start | bytes 884744 | tf_op jit(solution)/shard_map/ppermute | solution.py:64
  176.5 10.1 %collective-permute-start.2 = (bf16[2,288,256]{2,1,0:T(8,128)(2,1)S(1)}, bf16[2,288,256]{2,1,0:T(8,128)(2,1)S(1)}, u32[]{:S(2)}, u32[]{:S(2)}) collective-permute-start(bf16[2,288,256]{2,1,0:T(8,128)(2,1)S(1)} %collective-permute-done), channel_id=1, source_target_pairs={{0,7},{1,0},{2,1},{3,2},{4,3},{5,4},{6,5},{7,6},{8,15},{9,8},{10,9... | collective-permute-start | bytes 884744 | tf_op jit(solution)/shard_map/ppermute | solution.py:66
  184.7 8.7 %collective-permute-start.5 = (bf16[2,288,256]{2,1,0:T(8,128)(2,1)S(1)}, bf16[2,288,256]{2,1,0:T(8,128)(2,1)S(1)}, u32[]{:S(2)}, u32[]{:S(2)}) collective-permute-start(bf16[2,288,256]{2,1,0:T(8,128)(2,1)S(1)} %collective-permute-done.3), channel_id=1, source_target_pairs={{0,1},{1,2},{2,3},{3,4},{4,5},{5,6},{6,7},{7,0},{8,9},{9,10},{10,1... | collective-permute-start | bytes 884744 | tf_op jit(solution)/shard_map/ppermute | solution.py:64
  186.6 9.3 %collective-permute-start.4 = (bf16[2,288,256]{2,1,0:T(8,128)(2,1)S(1)}, bf16[2,288,256]{2,1,0:T(8,128)(2,1)S(1)}, u32[]{:S(2)}, u32[]{:S(2)}) collective-permute-start(bf16[2,288,256]{2,1,0:T(8,128)(2,1)S(1)} %collective-permute-done.2), channel_id=1, source_target_pairs={{0,7},{1,0},{2,1},{3,2},{4,3},{5,4},{6,5},{7,6},{8,15},{9,8},{10,9... | collective-permute-start | bytes 884744 | tf_op jit(solution)/shard_map/ppermute | solution.py:66
  193.4 10.0 %collective-permute-start.6 = (bf16[2,288,256]{2,1,0:T(8,128)(2,1)S(1)}, bf16[2,288,256]{2,1,0:T(8,128)(2,1)S(1)}, u32[]{:S(2)}, u32[]{:S(2)}) collective-permute-start(bf16[2,288,256]{2,1,0:T(8,128)(2,1)S(1)} %collective-permute-done.5), channel_id=1, source_target_pairs={{0,1},{1,2},{2,3},{3,4},{4,5},{5,6},{6,7},{7,0},{8,9},{9,10},{10,1... | collective-permute-start | bytes 884744 | tf_op jit(solution)/shard_map/ppermute | solution.py:64
Sparse Core Ops, SparseCore 0:
  14.2 102.1 all-gather.1
  123.1 40.5 reduce-scatter.1
